TPU v7x, 128 devices: a whole 4x4x4 slice. The times are simulated.
128 devices in a mesh: req: 16 (over z, x_hi, core), mdl: 8 (over x_lo, y).
Axes of the slice: x: 4 (x_hi: 2, x_lo: 2; x = x_hi * 2 + x_lo), y: 4, z: 4, core: 2. Of those that a mesh axis runs over, the one named last changes fastest.
Arguments:
- tokens: bfloat16 [16384, 2048], P('req'), may hold values from -6 to 6
- doc_ids: int32 [16384], P('req'), may hold values from 0 to 16383, as said below
- positions: int32 [16384], P('req'), may hold values from 0 to 1023, as said below
- attn_gain: float32 [2048], replicated, may hold values from 0.5 to 1.5
- mlp_gain: float32 [2048], replicated, may hold values from 0.5 to 1.5
- q_gain: float32 [128], replicated, may hold values from 0.5 to 48
- key_norm_gain: float32 [128], replicated, may hold values from 0.5 to 1.5
- q_weight: float32 [2048, 2048], P('req', 'mdl'), may hold values from -0.125 to 0.125
- key_matrix: float32 [2048, 1024], P('req', 'mdl'), may hold values from -0.125 to 0.125
- value_matrix: float32 [2048, 1024], P('req', 'mdl'), may hold values from -0.125 to 0.125
- o_weight: float32 [2048, 2048], P('mdl', 'req'), may hold values from -0.125 to 0.125
- gate_weight: float32 [2048, 6144], P('mdl', 'req'), may hold values from -0.125 to 0.125
- up_weight: float32 [2048, 6144], P('mdl', 'req'), may hold values from -0.125 to 0.125
- down_weight: float32 [6144, 2048], P('req', 'mdl'), may hold values from -0.078125 to 0.078125
Outputs:
- layer_out: bfloat16 [16384, 2048], P(('req', 'mdl'))
- key_value_cache: bfloat16 [2, 16384, 1024], P(None, 'req', 'mdl')
Inputs may be any that keep to these rules, and one draw needn't show every extreme that they name: `doc_ids`: A row's prompt number is the index of its prompt's first row among all packed rows, so it never falls along the rows; a prompt holds at most 1024 rows, every aligned block of 1024 rows has a prompt start in its second half, every block but the first begins inside the prompt that the block before it ends with, and the last row starts a prompt. `positions`: positions count from 0 at each prompt's first row.
All inputs are finite; a program needn't handle non-finite values.
Results may differ from a plain program's by a relative error of at most 0.02.
The roundings to bfloat16 on the way count: a program that leaves them out, or rounds other values in their place, can miss the bound.
Values may be sent and summed in bfloat16 or wider, within the bound.
No kernel may reach another device: no remote copies, remote signals or barrier semaphores. Data moves between devices by JAX's collectives and lax.ppermute only.
A program may use at most 128 MiB of HBM per device.

v0:
```python
import math
import jax
import jax.numpy as jnp
from jax import lax
from jax.sharding import PartitionSpec as P

HEAD_SIZE = 128


def passed_along(block, axis, distance):
    devices = range(lax.axis_size(axis))
    route = [(i - distance, i) for i in devices if i - distance in devices]
    return lax.ppermute(block, axis, route)


def root_mean_scale(values, gain):
    return values * lax.rsqrt(jnp.mean(values * values, axis=-1, keepdims=True) + 1e-06) * gain


def apply_rotary(tensor, position):
    half = tensor.shape[-1] // 2
    freq = jnp.exp(
        jnp.arange(half, dtype=jnp.float32) * (-2.0 * math.log(1000000.0) / tensor.shape[-1])
    )
    angle = position.astype(jnp.float32)[:, None] * freq[None, :]
    cosine = jnp.cos(angle)[:, None, :]
    sine = jnp.sin(angle)[:, None, :]
    front = tensor[..., :half]
    back = tensor[..., half:]
    return jnp.concatenate([front * cosine - back * sine, back * cosine + front * sine], axis=-1)


def per_device(
    tokens,
    doc_ids,
    positions,
    attn_gain,
    mlp_gain,
    q_gain,
    key_norm_gain,
    q_weight,
    key_matrix,
    value_matrix,
    o_weight,
    gate_weight,
    up_weight,
    down_weight,
):
    rows_here = tokens.shape[0]
    normed = root_mean_scale(tokens.astype(jnp.float32), attn_gain).astype(jnp.bfloat16)
    query_cols = q_weight.shape[1]
    kv_cols = key_matrix.shape[1]
    pieces = (
        lax.all_gather(q_weight.astype(jnp.bfloat16), "req", axis=0, tiled=True),
        lax.all_gather(key_matrix.astype(jnp.bfloat16), "req", axis=0, tiled=True),
        lax.all_gather(value_matrix.astype(jnp.bfloat16), "req", axis=0, tiled=True),
    )
    query_raw, unnormed_keys, unnormed_values = tuple(
        (jnp.dot(normed, piece, preferred_element_type=jnp.float32) for piece in pieces)
    )
    q_heads = query_cols // HEAD_SIZE
    kv_heads = kv_cols // HEAD_SIZE
    head_groups = q_heads // kv_heads
    query_rows = apply_rotary(
        root_mean_scale(query_raw.reshape(rows_here, q_heads, HEAD_SIZE), q_gain), positions
    ).astype(jnp.bfloat16)
    rotated_keys = (
        apply_rotary(
            root_mean_scale(unnormed_keys.reshape(rows_here, kv_heads, HEAD_SIZE), key_norm_gain),
            positions,
        )
        .astype(jnp.bfloat16)
        .reshape(rows_here, kv_cols)
    )
    projected_values = unnormed_values.astype(jnp.bfloat16)
    key_value_cache = jnp.stack([rotated_keys, projected_values])
    prior_keys, prior_values = passed_along((rotated_keys, projected_values), "req", 1)
    all_keys = jnp.concatenate([prior_keys, rotated_keys], axis=0).reshape(-1, kv_heads, HEAD_SIZE)
    all_values = jnp.concatenate([prior_values, projected_values], axis=0).reshape(
        -1, kv_heads, HEAD_SIZE
    )
    prior_index = jnp.arange(prior_keys.shape[0], dtype=jnp.int32)
    prior_live = prior_index >= rows_here - positions[0]
    grouped_queries = query_rows.reshape(rows_here, kv_heads, head_groups, HEAD_SIZE)
    block_rows = min(512, rows_here)
    scale = HEAD_SIZE ** (-0.5)
    outputs = []
    for block_index in range(rows_here // block_rows):
        lower = block_index * block_rows
        block_q = grouped_queries[lower : lower + block_rows]
        block_doc = doc_ids[lower : lower + block_rows]
        block_pos = positions[lower : lower + block_rows]
        scores = (
            jnp.einsum("qkrd,skd->krqs", block_q, all_keys, preferred_element_type=jnp.float32)
            * scale
        )
        earlier = (block_doc == doc_ids[0])[:, None] & prior_live[None, :]
        current = (doc_ids[None, :] == block_doc[:, None]) & (
            positions[None, :] <= block_pos[:, None]
        )
        allowed = jnp.concatenate([earlier, current], axis=1)
        scores = jnp.where(allowed[None, None], scores, -jnp.inf)
        top = jnp.max(scores, axis=-1, keepdims=True)
        expo = jnp.exp(scores - top)
        probs = (expo / jnp.sum(expo, axis=-1, keepdims=True)).astype(jnp.bfloat16)
        context_block = jnp.einsum(
            "krqs,skd->qkrd", probs, all_values, preferred_element_type=jnp.float32
        )
        outputs.append(context_block.astype(jnp.bfloat16).reshape(block_rows, q_heads * HEAD_SIZE))
    context = jnp.concatenate(outputs, axis=0)
    head_terms = jnp.dot(
        context,
        lax.all_gather(o_weight.astype(jnp.bfloat16), "req", axis=1, tiled=True),
        preferred_element_type=jnp.float32,
    )
    attn_rows = lax.psum_scatter(
        head_terms.astype(jnp.bfloat16), "mdl", scatter_dimension=0, tiled=True
    ).astype(jnp.float32)
    share = rows_here // lax.axis_size("mdl")
    own_rows = lax.dynamic_slice_in_dim(tokens, lax.axis_index("mdl") * share, share, 0)
    resid = lax.optimization_barrier(
        (own_rows.astype(jnp.float32) + attn_rows).astype(jnp.bfloat16)
    ).astype(jnp.float32)
    mlp_in = root_mean_scale(resid, mlp_gain).astype(jnp.bfloat16)
    gate_local = gate_weight.astype(jnp.bfloat16)
    up_local = up_weight.astype(jnp.bfloat16)
    down_local = down_weight.astype(jnp.bfloat16)
    gate_whole, up_whole = (
        lax.all_gather(gate_local, "req", axis=1, tiled=True),
        lax.all_gather(up_local, "req", axis=1, tiled=True),
    )
    down_whole = lax.all_gather(down_local, "req", axis=0, tiled=True)
    gate_server, up_server = (
        lax.all_to_all(gate_whole, "mdl", split_axis=1, concat_axis=0, tiled=True),
        lax.all_to_all(up_whole, "mdl", split_axis=1, concat_axis=0, tiled=True),
    )
    down_server = lax.all_to_all(down_whole, "mdl", split_axis=0, concat_axis=1, tiled=True)
    piece = lax.all_gather(mlp_in, "mdl", axis=0, tiled=True)
    gate = jnp.dot(piece, gate_server, preferred_element_type=jnp.float32)
    upper = jnp.dot(piece, up_server, preferred_element_type=jnp.float32)
    hidden = (jax.nn.silu(gate) * upper).astype(jnp.bfloat16)
    unit_terms = jnp.dot(hidden, down_server, preferred_element_type=jnp.float32)
    mlp_rows = lax.psum_scatter(
        unit_terms.astype(jnp.bfloat16), "mdl", scatter_dimension=0, tiled=True
    ).astype(jnp.float32)
    layer_out = (resid + mlp_rows).astype(jnp.bfloat16)
    return (layer_out, key_value_cache)


def solution(mesh):
    in_specs = (
        P("req", None),
        P("req"),
        P("req"),
        P(),
        P(),
        P(),
        P(),
        P("req", "mdl"),
        P("req", "mdl"),
        P("req", "mdl"),
        P("mdl", "req"),
        P("mdl", "req"),
        P("mdl", "req"),
        P("req", "mdl"),
    )
    out_specs = (P(("req", "mdl"), None), P(None, "req", "mdl"))
    return jax.shard_map(
        per_device, mesh=mesh, in_specs=in_specs, out_specs=out_specs, check_vma=False
    )
```

profile of v0, /device:TPU:1, one launch (start us, length us, event | category | flops | bytes accessed | tf_op | source)
XLA Modules:
  0.0 521.2 jit_solution(16136902884525856238)
XLA Ops:
  7.2 1.5 convert_element_type.107
  8.8 0.0 all-gather.9.cloned.1.call-start
  8.8 1.5 convert_element_type.116
  10.4 0.0 all-gather.13.cloned.1.call-start
  10.5 3.2 fusion
  13.7 0.2 copy-done
  13.9 1.0 fusion.2
  15.0 30.4 %all_gather.25 = bf16[2048,128]{1,0:T(8,128)(2,1)S(1)} all-gather(bf16[128,128]{1,0:T(8,128)(2,1)S(1)} %convert_element_type.105), channel_id=1, replica_groups=mesh['req'=16,'mdl'=8] {'req'}, dimensions={0}, use_global_device_ids=true | all-gather | bytes 557056 | tf_op jit(solution)/shard_map/all_gather | solution.py:55
  45.4 1.5 multiply_reduce_fusion.1
  46.9 0.2 copy.28
  47.2 0.2 multiply_bitcast_fusion
  47.4 2.4 fusion.26
  49.8 0.7 copy-done.4
  50.5 0.8 pad_maximum_fusion.3
  51.4 1.9 collective-permute-start.1
  53.3 23.4 %all_gather.24 = bf16[2048,128]{1,0:T(8,128)(2,1)S(1)} all-gather(bf16[128,128]{1,0:T(8,128)(2,1)S(1)} %convert_element_type.103), channel_id=1, replica_groups=mesh['req'=16,'mdl'=8] {'req'}, dimensions={0}, use_global_device_ids=true | all-gather | bytes 557056 | tf_op jit(solution)/shard_map/all_gather | solution.py:56
  76.7 4.1 convolution_convert_fusion.2
  80.9 3.5 collective-permute-start
  84.4 0.8 copy.34
  85.2 0.2 reduce-scatter.3.cloned.1.call-start
  85.5 0.5 slice.40
  86.0 0.5 slice.41
  86.5 3.0 multiply_cosine_fusion
  89.5 0.6 broadcast_compare_fusion.1
  90.8 0.5 broadcast_and_fusion.1
  91.3 1.2 compare_and_fusion.1
  92.5 0.8 pad_add_fusion
  93.3 4.8 multiply_reduce_fusion
  98.1 1.5 copy.29
  99.7 0.3 multiply_multiply_fusion
  100.1 1.7 subtract_convert_fusion
  101.8 2.9 fusion.5
  104.7 2.9 fusion.6
  107.6 2.0 fusion.3
  109.6 2.2 fusion.4
  111.8 3.9 fusion.11
  115.7 3.9 fusion.14
  119.7 4.5 convolution_convert_fusion
  124.2 0.0 all-gather.15.cloned.1.call-start
  124.3 0.8 copy.36
  125.1 0.0 all-gather.17.cloned.1.call-start
  125.2 0.7 convert_element_type.125
  125.9 31.1 %all-gather.13.cloned.1.call-done = bf16[256,6144]{0,1:T(8,128)(2,1)} async-done(((bf16[256,384]{0,1:T(8,128)(2,1)}), bf16[256,6144]{0,1:T(8,128)(2,1)}) %all-gather.13.cloned.1.call-update) | async-done | bytes 3145744 | tf_op jit(solution)/shard_map/all_gather | solution.py:129
  157.0 4.1 all-to-all-start
  161.2 81.4 %reduce-scatter.3.cloned.1.call-done = bf16[128,2048]{1,0:T(8,128)(2,1)} async-done(((bf16[1024,2048]{1,0:T(8,128)(2,1)}), bf16[128,2048]{1,0:T(8,128)(2,1)}) %reduce-scatter.3.cloned.1.call-update) | async-done | bytes 524304 | tf_op jit(solution)/shard_map/reduce_scatter | solution.py:116
  242.6 1.3 add_convert_fusion
  243.9 0.2 fusion.17
  244.1 0.6 copy-done.2
  244.7 1.0 fusion.19
  245.7 49.2 %all-gather.15.cloned.1.call-done = bf16[256,6144]{0,1:T(8,128)(2,1)} async-done(((bf16[256,384]{0,1:T(8,128)(2,1)}), bf16[256,6144]{0,1:T(8,128)(2,1)}) %all-gather.15.cloned.1.call-update) | async-done | bytes 3145744 | tf_op jit(solution)/shard_map/all_gather | solution.py:130
  295.0 4.5 all-to-all-start.1
  299.5 54.8 %all-gather.17.cloned.1.call-done = bf16[6144,256]{1,0:T(8,128)(2,1)} async-done(((bf16[384,256]{1,0:T(8,128)(2,1)}), bf16[6144,256]{1,0:T(8,128)(2,1)}) %all-gather.17.cloned.1.call-update) | async-done | bytes 3145744 | tf_op jit(solution)/shard_map/all_gather | solution.py:132
  354.2 4.6 all-to-all-start.2
  358.9 3.1 copy.35
  362.0 3.3 copy.37
  365.2 54.4 %all-to-all-done.2 = bf16[8,768,256]{2,1,0:T(8,128)(2,1)} async-done(((bf16[8,768,256]{2,1,0:T(8,128)(2,1)}), bf16[8,768,256]{2,1,0:T(8,128)(2,1)}, u32[]{:S(2)}, u32[]{:S(2)}) %all-to-all-start.2) | async-done | bytes 3145760 | tf_op jit(solution)/shard_map/all_to_all | solution.py:137
  419.6 4.7 copy.38
  424.3 15.7 %all-gather.11.cloned.1.call-done = bf16[1024,2048]{1,0:T(8,128)(2,1)} async-done(((bf16[128,2048]{1,0:T(8,128)(2,1)}), bf16[1024,2048]{1,0:T(8,128)(2,1)}) %all-gather.11.cloned.1.call-update) | async-done | bytes 4194320 | tf_op jit(solution)/shard_map/all_gather | solution.py:138
  440.0 8.2 %fusion.49 = f32[1024,768]{1,0:T(8,128)} fusion(bf16[1024,2048]{1,0:T(8,128)(2,1)} %all-gather.11.cloned.1.call-done, bf16[2048,768]{1,0:T(8,128)(2,1)} %bitcast.100), kind=kOutput, calls=%fused_computation.91 | convolution fusion | flops 3221225472 | bytes 10485760 | tf_op jit(solution)/shard_map/dot_general | solution.py:139
  448.2 12.2 %convolution_convert_fusion.1 = bf16[1024,2048]{1,0:T(8,128)(2,1)} fusion(bf16[768,2048]{0,1:T(8,128)(2,1)} %bitcast.101, f32[1024,768]{1,0:T(8,128)} %fusion.49, bf16[1024,2048]{1,0:T(8,128)(2,1)} %all-gather.11.cloned.1.call-done, bf16[2048,768]{1,0:T(8,128)(2,1)S(1)} %bitcast.99), kind=kOutput, calls=%fused_computation.22 | convolution fusion | flops 6449266688 | bytes 17825792 | tf_op jit(solution)/shard_map/dot_general | solution.py:142
  460.5 0.9 copy-done.6
  461.4 1.9 pad_maximum_fusion
  463.3 49.1 %reduce-scatter.5.cloned.1.call-done = bf16[128,2048]{1,0:T(8,128)(2,1)} async-done(((bf16[1024,2048]{1,0:T(8,128)(2,1)}), bf16[128,2048]{1,0:T(8,128)(2,1)}) %reduce-scatter.5.cloned.1.call-update) | async-done | bytes 524304 | tf_op jit(solution)/shard_map/reduce_scatter | solution.py:143
  512.4 2.0 fusion.20
  (60 shorter events, 0.5 us)
Async XLA Ops:
  7.2 6.5 %copy-start.10 = (f32[128,128]{1,0:T(8,128)S(1)}, f32[128,128]{1,0:T(8,128)}, u32[]{:S(2)}) copy-start(f32[128,128]{1,0:T(8,128)} %param.22) | copy-start | bytes 196612
  7.2 6.6 %copy-start.14 = (f32[2048]{0:T(1024)S(1)}, f32[2048]{0:T(1024)}, u32[]{:S(2)}) copy-start(f32[2048]{0:T(1024)} %param.17) | copy-start | bytes 24580
  7.2 86.1 %all-gather.7.cloned.1.call-start = ((), (), s32[]{:S(2)}) async-start(), calls=%async_computation.5 | async-start | bytes 1114112 | tf_op jit(solution)/shard_map/all_gather | solution.py:54
  8.8 110.9 %all-gather.9.cloned.1.call-start = ((), (), s32[]{:S(2)}) async-start(), calls=%async_computation.6 | async-start | bytes 1114112 | tf_op jit(solution)/shard_map/all_gather | solution.py:113
  10.4 146.6 %all-gather.13.cloned.1.call-start = ((), (), s32[]{:S(2)}) async-start(), calls=%async_computation.9 | async-start | bytes 3342336 | tf_op jit(solution)/shard_map/all_gather | solution.py:129
  10.4 3.5 copy-start
  14.9 30.5 %copy-start.1 = (bf16[1024,2048]{1,0:T(8,128)(2,1)}, bf16[1024,2048]{1,0:T(8,128)(2,1)S(1)}, u32[]{:S(2)}) copy-start(bf16[1024,2048]{1,0:T(8,128)(2,1)S(1)} %fusion.2) | copy-start | bytes 12582916
  14.9 32.2 %copy-start.12 = (s32[1024]{0:T(1024)S(1)}, s32[1024]{0:T(1024)}, u32[]{:S(2)}) copy-start(s32[1024]{0:T(1024)} %param.16) | copy-start | bytes 12292
  15.0 32.2 %copy-start.16 = (f32[128]{0:T(128)S(1)}, f32[128]{0:T(128)}, u32[]{:S(2)}) copy-start(f32[128]{0:T(128)} %param.20) | copy-start | bytes 1540
  45.4 7.9 %copy-start.11 = (f32[128,128]{1,0:T(8,128)S(1)}, f32[128,128]{1,0:T(8,128)}, u32[]{:S(2)}) copy-start(f32[128,128]{1,0:T(8,128)} %param.23) | copy-start | bytes 196612
  49.8 0.7 copy-start.4
  49.8 34.6 %copy-start.7 = (f32[256,384]{1,0:T(8,128)S(1)}, f32[256,384]{1,0:T(8,128)}, u32[]{:S(2)}) copy-start(f32[256,384]{1,0:T(8,128)} %param.25) | copy-start | bytes 1179652
  50.5 35.0 %copy-start.13 = (s32[1024]{0:T(1024)S(1)}, s32[1024]{0:T(1024)}, u32[]{:S(2)}) copy-start(s32[1024]{0:T(1024)} %param.15) | copy-start | bytes 12292
  51.4 50.4 %collective-permute-start.1 = (bf16[1024,128]{1,0:T(8,128)(2,1)}, bf16[1024,128]{1,0:T(8,128)(2,1)}, u32[]{:S(2)}, u32[]{:S(2)}) collective-permute-start(bf16[1024,128]{1,0:T(8,128)(2,1)} %pad_maximum_fusion.3), channel_id=1, source_target_pairs={{0,8},{8,16},{16,24},{24,32},{32,40},{40,48},{48,56},{56,64},{64,7... | collective-permute-start | bytes 786440 | tf_op jit(solution)/shard_map/ppermute | solution.py:13
  80.9 31.0 %collective-permute-start = (bf16[1024,128]{1,0:T(8,128)(2,1)}, bf16[1024,128]{1,0:T(8,128)(2,1)}, u32[]{:S(2)}, u32[]{:S(2)}) collective-permute-start(bf16[1024,128]{1,0:T(8,128)(2,1)} %convolution_convert_fusion.2), channel_id=1, source_target_pairs={{0,8},{8,16},{16,24},{24,32},{32,40},{40,48},{48,56},{56,64},{64,7... | collective-permute-start | bytes 786440 | tf_op jit(solution)/shard_map/ppermute | solution.py:13
  85.2 157.4 %reduce-scatter.3.cloned.1.call-start = ((), (), s32[]{:S(2)}) async-start(), calls=%async_computation.7 | async-start | bytes 4718592 | tf_op jit(solution)/shard_map/reduce_scatter | solution.py:116
  93.3 6.5 %copy-start.17 = (f32[128]{0:T(128)S(1)}, f32[128]{0:T(128)}, u32[]{:S(2)}) copy-start(f32[128]{0:T(128)} %param.19) | copy-start | bytes 1540
  99.7 2.1 copy-start.5
  119.7 4.6 copy-start.8
  124.2 1.0 copy-start.9
  124.2 170.8 %all-gather.15.cloned.1.call-start = ((), (), s32[]{:S(2)}) async-start(), calls=%async_computation.10 | async-start | bytes 3342336 | tf_op jit(solution)/shard_map/all_gather | solution.py:130
  125.1 229.1 %all-gather.17.cloned.1.call-start = ((), (), s32[]{:S(2)}) async-start(), calls=%async_computation.11 | async-start | bytes 3342336 | tf_op jit(solution)/shard_map/all_gather | solution.py:132
  157.0 87.7 %copy-start.15 = (f32[2048]{0:T(1024)S(1)}, f32[2048]{0:T(1024)}, u32[]{:S(2)}) copy-start(f32[2048]{0:T(1024)} %param.18) | copy-start | bytes 24580
  157.0 138.0 %all-to-all-start = ((bf16[256,8,768]{0,2,1:T(8,128)(2,1)}), bf16[256,8,768]{0,2,1:T(8,128)(2,1)S(1)}, u32[]{:S(2)}, u32[]{:S(2)}) async-start(bf16[256,8,768]{0,2,1:T(8,128)(2,1)} %bitcast.96), calls=%async_computation.1 | async-start | bytes 6291456 | tf_op jit(solution)/shard_map/all_to_all | solution.py:134
  161.2 278.8 %all-gather.11.cloned.1.call-start = ((), (), s32[]{:S(2)}) async-start(), calls=%async_computation.8 | async-start | bytes 4718592 | tf_op jit(solution)/shard_map/all_gather | solution.py:138
  243.9 0.8 copy-start.2
  295.0 59.3 %all-to-all-start.1 = ((bf16[256,8,768]{0,2,1:T(8,128)(2,1)}), bf16[256,8,768]{0,2,1:T(8,128)(2,1)}, u32[]{:S(2)}, u32[]{:S(2)}) async-start(bf16[256,8,768]{0,2,1:T(8,128)(2,1)} %bitcast.98), calls=%async_computation.2 | async-start | bytes 6291456 | tf_op jit(solution)/shard_map/all_to_all | solution.py:135
  354.2 65.3 %all-to-all-start.2 = ((bf16[8,768,256]{2,1,0:T(8,128)(2,1)}), bf16[8,768,256]{2,1,0:T(8,128)(2,1)}, u32[]{:S(2)}, u32[]{:S(2)}) async-start(bf16[8,768,256]{2,1,0:T(8,128)(2,1)} %bitcast.97), calls=%async_computation.3 | async-start | bytes 6291456 | tf_op jit(solution)/shard_map/all_to_all | solution.py:137
  358.8 153.6 %reduce-scatter.5.cloned.1.call-start = ((), (), s32[]{:S(2)}) async-start(), calls=%async_computation.12 | async-start | bytes 4718592 | tf_op jit(solution)/shard_map/reduce_scatter | solution.py:143
  460.4 0.9 copy-start.6
  460.4 52.0 %copy-start.3 = (bf16[128,2048]{1,0:T(8,128)(2,1)S(1)}, bf16[128,2048]{1,0:T(8,128)(2,1)}, u32[]{:S(2)}) copy-start(bf16[128,2048]{1,0:T(8,128)(2,1)} %copy-done.2) | copy-start | bytes 1572868
Sparse Core Ops, SparseCore 0:
  10.5 48.5 all-gather.6
  61.5 42.2 all-gather.8
  106.2 50.8 all-gather.12
  159.3 83.2 reduce-scatter.2
  244.9 50.0 all-gather.14
  297.3 56.8 all-gather.16
  356.5 83.5 all-gather.10
  460.6 51.7 reduce-scatter.4
where the time goes:
time: 522 us; the launch traced here: 521 us
  waiting for transfers between devices  336 us (64%)
  blocking collectives  53.9 us (10%)
  matrix products  49.1 us (9%)
  other arithmetic  30.2 us (6%)
  starting transfers between devices  19.1 us (4%)
  local copies, waits for them, and re-layouts  17.9 us (3%)
  between operations  15.1 us (3%)
    reduce_scatter x1, waiting for transfers between devices, per_device(): lax.psum_scatter(head_terms.astype(jnp.bfloat16), 'mdl', scatter_dimensio...  81.4 us
    all_gather x1, waiting for transfers between devices, per_device(): down_whole = lax.all_gather(down_local, 'req', axis=0, tiled=True)  54.8 us
    all_to_all x1, waiting for transfers between devices, per_device(): lax.all_to_all(down_whole, 'mdl', split_axis=0, concat_axis=1, tiled=True)  54.4 us
    all_gather x1, waiting for transfers between devices, per_device(): lax.all_gather(up_local, 'req', axis=1, tiled=True)  49.2 us
    reduce_scatter x1, waiting for transfers between devices, per_device(): lax.psum_scatter(unit_terms.astype(jnp.bfloat16), 'mdl', scatter_dimensio...  49.1 us
    all_gather x1, waiting for transfers between devices, per_device(): lax.all_gather(gate_local, 'req', axis=1, tiled=True)  31.1 us
    all_gather x1, blocking collectives, per_device(): lax.all_gather(key_matrix.astype(jnp.bfloat16), 'req', axis=0, tiled=True)  30.4 us
    all_gather x1, blocking collectives, per_device(): lax.all_gather(value_matrix.astype(jnp.bfloat16), 'req', axis=0, tiled=True)  23.4 us
  transfers between devices with their start and end apart: 13, of which 7 were waited for; matrix products, arithmetic and copies ran while one was open for 14% of the time, Pallas kernels for 0%

commit v1 on v0

--- a/solution.py
+++ b/solution.py
@@ -134,7 +134,10 @@
         lax.all_to_all(gate_whole, "mdl", split_axis=1, concat_axis=0, tiled=True),
         lax.all_to_all(up_whole, "mdl", split_axis=1, concat_axis=0, tiled=True),
     )
-    down_server = lax.all_to_all(down_whole, "mdl", split_axis=0, concat_axis=1, tiled=True)
+    down_server = jnp.concatenate(
+        lax.all_to_all(jnp.stack(jnp.split(down_whole, lax.axis_size("mdl"), axis=0)), "mdl", 0, 0),
+        axis=1,
+    )
     piece = lax.all_gather(mlp_in, "mdl", axis=0, tiled=True)
     gate = jnp.dot(piece, gate_server, preferred_element_type=jnp.float32)
     upper = jnp.dot(piece, up_server, preferred_element_type=jnp.float32)

time: 522 us -> 532 us (1.019)
  local copies, waits for them, and re-layouts: 17.9 us -> 28.1 us
    all_to_all x1, waiting for transfers between devices: 54.4 us -> 0.01 us  [per_device(): lax.all_to_all(jnp.stack(jnp.split(down_whole, lax.axis_size('mdl'), axis...]
    all_gather x1, waiting for transfers between devices: 15.7 us -> 66.9 us  [per_device(): piece = lax.all_gather(mlp_in, 'mdl', axis=0, tiled=True)]
    unnamed x38 -> x46, local copies, waits for them, and re-layouts: 4.06 us -> 17.3 us
  transfers between devices with their start and end apart: 13 -> 13, of which waited for: 7 -> 6; matrix products, arithmetic and copies ran while one was open for 14% -> 17% of each run, Pallas kernels for 0% -> 0%
where the time goes in v1:
time: 532 us; the launch traced here: 531 us
  waiting for transfers between devices  336 us (63%)
  blocking collectives  53.9 us (10%)
  matrix products  49.3 us (9%)
  other arithmetic  29.5 us (6%)
  local copies, waits for them, and re-layouts  28.1 us (5%)
  starting transfers between devices  19.2 us (4%)
  between operations  15.2 us (3%)
    reduce_scatter x1, waiting for transfers between devices, per_device(): lax.psum_scatter(head_terms.astype(jnp.bfloat16), 'mdl', scatter_dimensio...  81.4 us
    all_gather x1, waiting for transfers between devices, per_device(): piece = lax.all_gather(mlp_in, 'mdl', axis=0, tiled=True)  66.9 us
    all_gather x1, waiting for transfers between devices, per_device(): down_whole = lax.all_gather(down_local, 'req', axis=0, tiled=True)  55.4 us
    reduce_scatter x1, waiting for transfers between devices, per_device(): lax.psum_scatter(unit_terms.astype(jnp.bfloat16), 'mdl', scatter_dimensio...  51.7 us
    all_gather x1, waiting for transfers between devices, per_device(): lax.all_gather(up_local, 'req', axis=1, tiled=True)  49.2 us
    all_gather x1, waiting for transfers between devices, per_device(): lax.all_gather(gate_local, 'req', axis=1, tiled=True)  30.9 us
    all_gather x1, blocking collectives, per_device(): lax.all_gather(key_matrix.astype(jnp.bfloat16), 'req', axis=0, tiled=True)  30.5 us
    all_gather x1, blocking collectives, per_device(): lax.all_gather(value_matrix.astype(jnp.bfloat16), 'req', axis=0, tiled=True)  23.4 us
  transfers between devices with their start and end apart: 13, of which 6 were waited for; matrix products, arithmetic and copies ran while one was open for 17% of the time, Pallas kernels for 0%

profile of v1, /device:TPU:1, one launch (start us, length us, event | category | flops | bytes accessed | tf_op | source)
XLA Modules:
  0.0 530.7 jit_solution(4713531751264445141)
XLA Ops:
  7.2 1.5 convert_element_type.107
  8.8 1.5 convert_element_type.116
  10.5 3.2 fusion
  13.9 1.0 fusion.2
  15.0 30.5 %all_gather.25 = bf16[2048,128]{1,0:T(8,128)(2,1)S(1)} all-gather(bf16[128,128]{1,0:T(8,128)(2,1)S(1)} %convert_element_type.105), channel_id=1, replica_groups=mesh['req'=16,'mdl'=8] {'req'}, dimensions={0}, use_global_device_ids=true | all-gather | bytes 557056 | tf_op jit(solution)/shard_map/all_gather | solution.py:55
  45.4 1.5 multiply_reduce_fusion.1
  47.0 0.2 copy.29
  47.2 0.2 multiply_bitcast_fusion
  47.4 2.4 fusion.26
  49.9 0.7 copy-done.4
  50.6 0.9 pad_maximum_fusion.3
  51.4 1.9 collective-permute-start.1
  53.4 23.4 %all_gather.24 = bf16[2048,128]{1,0:T(8,128)(2,1)S(1)} all-gather(bf16[128,128]{1,0:T(8,128)(2,1)S(1)} %convert_element_type.103), channel_id=1, replica_groups=mesh['req'=16,'mdl'=8] {'req'}, dimensions={0}, use_global_device_ids=true | all-gather | bytes 557056 | tf_op jit(solution)/shard_map/all_gather | solution.py:56
  76.7 4.1 convolution_convert_fusion.2
  80.9 3.6 collective-permute-start
  84.5 0.8 copy.35
  85.3 0.2 reduce-scatter.3.cloned.1.call-start
  85.6 0.5 slice.40
  86.1 0.5 slice.41
  86.6 3.0 multiply_cosine_fusion
  89.6 0.6 broadcast_compare_fusion.1
  90.9 0.5 broadcast_and_fusion.1
  91.4 1.2 compare_and_fusion.1
  92.6 0.8 pad_add_fusion
  93.4 4.8 multiply_reduce_fusion
  98.3 1.5 copy.30
  99.9 0.3 multiply_multiply_fusion
  100.2 1.7 subtract_convert_fusion
  101.9 2.9 fusion.5
  104.8 2.9 fusion.6
  107.8 2.0 fusion.3
  109.8 2.2 fusion.4
  112.0 3.9 fusion.11
  115.9 3.9 fusion.14
  119.8 4.5 convolution_convert_fusion
  124.4 0.8 copy.37
  125.3 0.8 copy.39
  126.2 30.9 %all-gather.13.cloned.1.call-done = bf16[256,6144]{0,1:T(8,128)(2,1)} async-done(((bf16[256,384]{0,1:T(8,128)(2,1)}), bf16[256,6144]{0,1:T(8,128)(2,1)}) %all-gather.13.cloned.1.call-update) | async-done | bytes 3145744 | tf_op jit(solution)/shard_map/all_gather | solution.py:129
  157.1 4.1 all-to-all-start
  161.3 81.4 %reduce-scatter.3.cloned.1.call-done = bf16[128,2048]{1,0:T(8,128)(2,1)} async-done(((bf16[1024,2048]{1,0:T(8,128)(2,1)}), bf16[128,2048]{1,0:T(8,128)(2,1)}) %reduce-scatter.3.cloned.1.call-update) | async-done | bytes 524304 | tf_op jit(solution)/shard_map/reduce_scatter | solution.py:116
  242.6 1.3 add_convert_fusion
  244.2 0.6 copy-done.2
  244.8 1.0 fusion.19
  245.8 49.2 %all-gather.15.cloned.1.call-done = bf16[256,6144]{0,1:T(8,128)(2,1)} async-done(((bf16[256,384]{0,1:T(8,128)(2,1)}), bf16[256,6144]{0,1:T(8,128)(2,1)}) %all-gather.15.cloned.1.call-update) | async-done | bytes 3145744 | tf_op jit(solution)/shard_map/all_gather | solution.py:130
  295.0 4.5 all-to-all-start.1
  299.5 55.4 %all-gather.17.cloned.1.call-done = bf16[6144,256]{0,1:T(8,128)(2,1)} async-done(((bf16[384,256]{0,1:T(8,128)(2,1)}), bf16[6144,256]{0,1:T(8,128)(2,1)}) %all-gather.17.cloned.1.call-update) | async-done | bytes 3145744 | tf_op jit(solution)/shard_map/all_gather | solution.py:132
  354.9 1.8 fusion.39
  356.6 1.8 fusion.38
  358.4 1.8 fusion.37
  360.2 1.8 fusion.36
  362.0 1.8 fusion.35
  363.7 1.8 fusion.34
  365.5 1.8 fusion.33
  367.3 1.8 fusion.32
  369.0 4.6 all-to-all-start.2
  373.7 3.1 copy.36
  376.8 3.2 copy.38
  379.9 66.9 %all-gather.11.cloned.1.call-done = bf16[1024,2048]{1,0:T(8,128)(2,1)} async-done(((bf16[128,2048]{1,0:T(8,128)(2,1)}), bf16[1024,2048]{1,0:T(8,128)(2,1)}) %all-gather.11.cloned.1.call-update) | async-done | bytes 4194320 | tf_op jit(solution)/shard_map/all_gather | solution.py:141
  446.8 8.2 %fusion.57 = f32[1024,768]{1,0:T(8,128)} fusion(bf16[1024,2048]{1,0:T(8,128)(2,1)} %all-gather.11.cloned.1.call-done, bf16[2048,768]{1,0:T(8,128)(2,1)} %bitcast.131), kind=kOutput, calls=%fused_computation.107 | convolution fusion | flops 3221225472 | bytes 10485760 | tf_op jit(solution)/shard_map/dot_general | solution.py:142
  455.1 12.3 %convolution_convert_fusion.1 = bf16[1024,2048]{1,0:T(8,128)(2,1)} fusion(bf16[768,2048]{0,1:T(8,128)(2,1)} %bitcast.36, f32[1024,768]{1,0:T(8,128)} %fusion.57, bf16[1024,2048]{1,0:T(8,128)(2,1)} %all-gather.11.cloned.1.call-done, bf16[2048,768]{1,0:T(8,128)(2,1)S(1)} %bitcast.130), kind=kOutput, calls=%fused_computation.22 | convolution fusion | flops 6449266688 | bytes 17825792 | tf_op jit(solution)/shard_map/dot_general | solution.py:145
  467.4 0.9 copy-done.6
  468.3 1.9 pad_maximum_fusion
  470.2 51.7 %reduce-scatter.5.cloned.1.call-done = bf16[128,2048]{1,0:T(8,128)(2,1)} async-done(((bf16[1024,2048]{1,0:T(8,128)(2,1)}), bf16[128,2048]{1,0:T(8,128)(2,1)}) %reduce-scatter.5.cloned.1.call-update) | async-done | bytes 524304 | tf_op jit(solution)/shard_map/reduce_scatter | solution.py:146
  521.9 2.0 fusion.20
  (67 shorter events, 1.0 us)
Async XLA Ops:
  7.2 6.5 %copy-start.10 = (f32[128,128]{1,0:T(8,128)S(1)}, f32[128,128]{1,0:T(8,128)}, u32[]{:S(2)}) copy-start(f32[128,128]{1,0:T(8,128)} %param.22) | copy-start | bytes 196612
  7.2 6.5 %copy-start.14 = (f32[2048]{0:T(1024)S(1)}, f32[2048]{0:T(1024)}, u32[]{:S(2)}) copy-start(f32[2048]{0:T(1024)} %param.17) | copy-start | bytes 24580
  7.2 86.2 %all-gather.7.cloned.1.call-start = ((), (), s32[]{:S(2)}) async-start(), calls=%async_computation.5 | async-start | bytes 1114112 | tf_op jit(solution)/shard_map/all_gather | solution.py:54
  8.8 111.0 %all-gather.9.cloned.1.call-start = ((), (), s32[]{:S(2)}) async-start(), calls=%async_computation.6 | async-start | bytes 1114112 | tf_op jit(solution)/shard_map/all_gather | solution.py:113
  10.4 146.7 %all-gather.13.cloned.1.call-start = ((), (), s32[]{:S(2)}) async-start(), calls=%async_computation.9 | async-start | bytes 3342336 | tf_op jit(solution)/shard_map/all_gather | solution.py:129
  10.4 3.5 copy-start
  14.9 30.5 %copy-start.1 = (bf16[1024,2048]{1,0:T(8,128)(2,1)}, bf16[1024,2048]{1,0:T(8,128)(2,1)S(1)}, u32[]{:S(2)}) copy-start(bf16[1024,2048]{1,0:T(8,128)(2,1)S(1)} %fusion.2) | copy-start | bytes 12582916
  14.9 32.3 %copy-start.12 = (s32[1024]{0:T(1024)S(1)}, s32[1024]{0:T(1024)}, u32[]{:S(2)}) copy-start(s32[1024]{0:T(1024)} %param.16) | copy-start | bytes 12292
  14.9 32.3 %copy-start.16 = (f32[128]{0:T(128)S(1)}, f32[128]{0:T(128)}, u32[]{:S(2)}) copy-start(f32[128]{0:T(128)} %param.20) | copy-start | bytes 1540
  45.4 7.9 %copy-start.11 = (f32[128,128]{1,0:T(8,128)S(1)}, f32[128,128]{1,0:T(8,128)}, u32[]{:S(2)}) copy-start(f32[128,128]{1,0:T(8,128)} %param.23) | copy-start | bytes 196612
  49.9 0.7 copy-start.4
  49.9 34.6 %copy-start.7 = (f32[256,384]{1,0:T(8,128)S(1)}, f32[256,384]{1,0:T(8,128)}, u32[]{:S(2)}) copy-start(f32[256,384]{1,0:T(8,128)} %param.25) | copy-start | bytes 1179652
  50.6 35.0 %copy-start.13 = (s32[1024]{0:T(1024)S(1)}, s32[1024]{0:T(1024)}, u32[]{:S(2)}) copy-start(s32[1024]{0:T(1024)} %param.15) | copy-start | bytes 12292
  51.4 50.4 %collective-permute-start.1 = (bf16[1024,128]{1,0:T(8,128)(2,1)}, bf16[1024,128]{1,0:T(8,128)(2,1)}, u32[]{:S(2)}, u32[]{:S(2)}) collective-permute-start(bf16[1024,128]{1,0:T(8,128)(2,1)} %pad_maximum_fusion.3), channel_id=1, source_target_pairs={{0,8},{8,16},{16,24},{24,32},{32,40},{40,48},{48,56},{56,64},{64,7... | collective-permute-start | bytes 786440 | tf_op jit(solution)/shard_map/ppermute | solution.py:13
  80.9 31.1 %collective-permute-start = (bf16[1024,128]{1,0:T(8,128)(2,1)}, bf16[1024,128]{1,0:T(8,128)(2,1)}, u32[]{:S(2)}, u32[]{:S(2)}) collective-permute-start(bf16[1024,128]{1,0:T(8,128)(2,1)} %convolution_convert_fusion.2), channel_id=1, source_target_pairs={{0,8},{8,16},{16,24},{24,32},{32,40},{40,48},{48,56},{56,64},{64,7... | collective-permute-start | bytes 786440 | tf_op jit(solution)/shard_map/ppermute | solution.py:13
  85.3 157.3 %reduce-scatter.3.cloned.1.call-start = ((), (), s32[]{:S(2)}) async-start(), calls=%async_computation.7 | async-start | bytes 4718592 | tf_op jit(solution)/shard_map/reduce_scatter | solution.py:116
  93.4 6.5 %copy-start.17 = (f32[128]{0:T(128)S(1)}, f32[128]{0:T(128)}, u32[]{:S(2)}) copy-start(f32[128]{0:T(128)} %param.19) | copy-start | bytes 1540
  99.8 2.1 copy-start.5
  119.8 4.6 copy-start.8
  124.3 1.0 copy-start.9
  124.4 170.6 %all-gather.15.cloned.1.call-start = ((), (), s32[]{:S(2)}) async-start(), calls=%async_computation.10 | async-start | bytes 3342336 | tf_op jit(solution)/shard_map/all_gather | solution.py:130
  125.3 229.6 %all-gather.17.cloned.1.call-start = ((), (), s32[]{:S(2)}) async-start(), calls=%async_computation.11 | async-start | bytes 3342336 | tf_op jit(solution)/shard_map/all_gather | solution.py:132
  157.1 87.7 %copy-start.15 = (f32[2048]{0:T(1024)S(1)}, f32[2048]{0:T(1024)}, u32[]{:S(2)}) copy-start(f32[2048]{0:T(1024)} %param.18) | copy-start | bytes 24580
  157.1 138.0 %all-to-all-start = ((bf16[256,8,768]{0,2,1:T(8,128)(2,1)}), bf16[256,8,768]{0,2,1:T(8,128)(2,1)S(1)}, u32[]{:S(2)}, u32[]{:S(2)}) async-start(bf16[256,8,768]{0,2,1:T(8,128)(2,1)} %bitcast.128), calls=%async_computation.1 | async-start | bytes 6291456 | tf_op jit(solution)/shard_map/all_to_all | solution.py:134
  161.2 285.6 %all-gather.11.cloned.1.call-start = ((), (), s32[]{:S(2)}) async-start(), calls=%async_computation.8 | async-start | bytes 4718592 | tf_op jit(solution)/shard_map/all_gather | solution.py:141
  244.0 0.8 copy-start.2
  295.0 74.0 %all-to-all-start.1 = ((bf16[256,8,768]{0,2,1:T(8,128)(2,1)}), bf16[256,8,768]{0,2,1:T(8,128)(2,1)}, u32[]{:S(2)}, u32[]{:S(2)}) async-start(bf16[256,8,768]{0,2,1:T(8,128)(2,1)} %bitcast.129), calls=%async_computation.2 | async-start | bytes 6291456 | tf_op jit(solution)/shard_map/all_to_all | solution.py:135
  369.0 86.0 %all-to-all-start.2 = ((bf16[8,768,256]{1,2,0:T(8,128)(2,1)}), bf16[8,768,256]{1,2,0:T(8,128)(2,1)}, u32[]{:S(2)}, u32[]{:S(2)}) async-start(bf16[8,768,256]{1,2,0:T(8,128)(2,1)} %fusion.32), calls=%async_computation.3 | async-start | bytes 6291456 | tf_op jit(solution)/shard_map/all_to_all | solution.py:138
  373.6 148.3 %reduce-scatter.5.cloned.1.call-start = ((), (), s32[]{:S(2)}) async-start(), calls=%async_computation.12 | async-start | bytes 4718592 | tf_op jit(solution)/shard_map/reduce_scatter | solution.py:146
  467.4 0.9 copy-start.6
  467.4 54.5 %copy-start.3 = (bf16[128,2048]{1,0:T(8,128)(2,1)S(1)}, bf16[128,2048]{1,0:T(8,128)(2,1)}, u32[]{:S(2)}) copy-start(bf16[128,2048]{1,0:T(8,128)(2,1)} %copy-done.2) | copy-start | bytes 1572868
Sparse Core Ops, SparseCore 0:
  10.5 48.5 all-gather.6
  61.5 42.2 all-gather.8
  106.2 50.8 all-gather.12
  159.3 83.2 reduce-scatter.2
  244.9 50.0 all-gather.14
  297.2 57.6 all-gather.16
  357.1 89.6 all-gather.10
  467.5 54.3 reduce-scatter.4
